TPU v7x, 256 devices: a whole 4x4x8 slice. The times are simulated.
256 devices in a mesh: kgrp: 16 (over y, z_hi, core), wrow: 16 (over z_lo, x).
Axes of the slice: x: 4, y: 4, z: 8 (z_hi: 2, z_lo: 4; z = z_hi * 4 + z_lo), core: 2. Of those that a mesh axis runs over, the one named last changes fastest.
Arguments:
- orbitals: bfloat16 [16, 1024, 384], P('kgrp', 'wrow'), may hold values from -0.71875 to 0.71875
- energies: float32 [16, 192], replicated, may hold values from -2 to 2
- perm_table: int32 [64, 16], replicated, may hold values from 0 to 15, each once within a row
- momenta: int32 [2], replicated, may hold values from 0 to 63
- screened_w: bfloat16 [2, 2, 16, 1024, 1024], P(None, None, None, 'wrow'), may hold values from -6 to 6
Outputs:
- sigma: float32 [16, 16, 192, 384], P('kgrp', None, 'wrow')
Inputs may be any that keep to these rules, and one draw needn't show every extreme that they name: `perm_table`: each row is a permutation of the 16 k-points: entry k names the k-point k minus that row's momentum transfer. `momenta`: each entry names a row of perm_table; the two may coincide.
All inputs are finite; a program needn't handle non-finite values.
Results may differ from a plain program's by a relative error of at most 0.0055.
Values may be sent and summed in bfloat16 or wider, within the bound.
A program may use at most 128 MiB of HBM per device.

v0:
```python
import jax
import jax.numpy as jnp
from jax import lax
from jax.sharding import PartitionSpec as P

BETA = 8.0


def from_everyone(array, axis):
    devices = lax.axis_size(axis)
    return lax.all_to_all(
        jnp.broadcast_to(array[None], (devices, *array.shape)), axis, 0, 0, tiled=True
    )


def in_order(tiles, dim):
    tiles = jnp.moveaxis(tiles, 0, dim)
    shape = tiles.shape
    return tiles.reshape(*shape[:dim], shape[dim] * shape[dim + 1], *shape[dim + 2 :])


def gathered_copies(array, axis, dim):
    tiles = from_everyone(array, axis)
    return in_order(tiles, dim)


def occupation(energy_row, tau_count):
    tau_grid = BETA * (jnp.arange(tau_count, dtype=jnp.float32) + 0.5) / tau_count
    return -jnp.exp(
        -tau_grid[:, None] * energy_row[None, :] - jax.nn.softplus(-BETA * energy_row)[None, :]
    )


def rotate(matrix):
    middle = matrix.shape[-1] // 2
    return jnp.concatenate([-matrix[..., middle:], matrix[..., :middle]], axis=-1)


def scaled_rows(point_rows, factor):
    doubled = jnp.concatenate([factor, factor], axis=1)
    return (point_rows.astype(jnp.float32)[None] * doubled[:, None, :]).astype(jnp.bfloat16)


def shards(orbitals, energies, perm_table, momenta, screened_w):
    own_rows = orbitals[0]
    group_index = lax.axis_index("kgrp")
    tau_count = screened_w.shape[2]
    point_rows = own_rows.shape[0]
    row_width = own_rows.shape[1]
    orbital_count = row_width // 2
    whole_own = gathered_copies(own_rows, "wrow", 0)
    halves = []
    for q_slot in range(screened_w.shape[0]):
        source = perm_table[momenta[q_slot], group_index]
        shard_piece = gathered_copies(own_rows, "kgrp", 0)
        piece_rows = shard_piece.shape[0]
        offset = source * point_rows
        inside = (offset >= 0) & (offset + point_rows <= piece_rows)
        chosen = lax.dynamic_slice_in_dim(
            shard_piece, jnp.clip(offset, 0, piece_rows - point_rows), point_rows, 0
        )
        remote = jnp.where(inside, chosen, jnp.zeros_like(own_rows))
        factor = occupation(energies[source], tau_count)
        flat_left = scaled_rows(remote, factor).reshape(-1, row_width)
        columns_shard_piece = gathered_copies(remote, "wrow", 0)
        green_real = jnp.dot(flat_left, columns_shard_piece.T, preferred_element_type=jnp.float32)
        green_imag = jnp.dot(
            flat_left, rotate(columns_shard_piece).T, preferred_element_type=jnp.float32
        )
        greens = jnp.stack([green_real, green_imag])
        w_slice = screened_w[q_slot].reshape(2, -1, screened_w.shape[-1]).astype(jnp.float32)
        screen_real = (greens[0] * w_slice[0] - greens[1] * w_slice[1]).astype(jnp.bfloat16)
        screen_imag = (greens[0] * w_slice[1] + greens[1] * w_slice[0]).astype(jnp.bfloat16)
        half_proj = (
            jnp.dot(screen_real, whole_own, preferred_element_type=jnp.float32)
            + jnp.dot(screen_imag, rotate(whole_own), preferred_element_type=jnp.float32)
        ).astype(jnp.bfloat16)
        halves.append(half_proj.reshape(tau_count, point_rows, 2, orbital_count))
    swapped = lax.all_to_all(jnp.stack(halves), "wrow", split_axis=4, concat_axis=2, tiled=True)
    blocks = jnp.einsum(
        "pi,qtpcj->ticj", whole_own.astype(jnp.float32), swapped.astype(jnp.float32)
    )
    real_part = blocks[:, :orbital_count, 0] + blocks[:, orbital_count:, 1]
    imag_part = blocks[:, :orbital_count, 1] - blocks[:, orbital_count:, 0]
    column_block = jnp.stack([real_part, imag_part], axis=2)
    row_block = lax.all_to_all(column_block, "wrow", split_axis=1, concat_axis=3, tiled=True)
    sigma_sum = row_block.reshape(tau_count, row_block.shape[1], row_width)
    return sigma_sum[None]


def solution(mesh):
    return jax.shard_map(
        shards,
        mesh=mesh,
        in_specs=(P("kgrp", "wrow", None), P(), P(), P(), P(None, None, None, "wrow", None)),
        out_specs=P("kgrp", None, "wrow", None),
        check_vma=False,
    )
```

profile of v0, /device:TPU:16, one launch (start us, length us, event | category | flops | bytes accessed | tf_op | source)
XLA Modules:
  0.0 221.0 jit_solution(9754906954036779875)
XLA Ops:
  0.0 1.9 broadcast_in_dim.9
  1.9 11.4 %all-to-all-start = ((bf16[16,64,384]{2,1,0:T(8,128)(2,1)}), bf16[16,64,384]{2,1,0:T(8,128)(2,1)S(1)}, u32[]{:S(2)}, u32[]{:S(2)}) async-start(bf16[16,64,384]{2,1,0:T(8,128)(2,1)} %broadcast_in_dim.9), calls=%async_computation | async-start | bytes 1572864 | tf_op jit(solution)/shard_map/all_to_all | solution.py:11
  17.7 1.4 fusion.25
  25.0 5.7 %all-to-all-done = bf16[16,64,384]{2,1,0:T(8,128)(2,1)S(1)} async-done(((bf16[16,64,384]{2,1,0:T(8,128)(2,1)}), bf16[16,64,384]{2,1,0:T(8,128)(2,1)S(1)}, u32[]{:S(2)}, u32[]{:S(2)}) %all-to-all-start) | async-done | bytes 786464 | tf_op jit(solution)/shard_map/all_to_all | solution.py:11
  30.7 11.4 %all-to-all-start.2 = ((bf16[16,64,384]{2,1,0:T(8,128)(2,1)}), bf16[16,64,384]{2,1,0:T(8,128)(2,1)S(1)}, u32[]{:S(2)}, u32[]{:S(2)}) async-start(bf16[16,64,384]{2,1,0:T(8,128)(2,1)} %broadcast_in_dim.9), calls=%async_computation.2 | async-start | bytes 1572864 | tf_op jit(solution)/shard_map/all_to_all | solution.py:11
  42.1 11.4 %slice_convert_fusion.1 = (f32[1,2,16,64,1024]{4,3,2,1,0:T(8,128)}, f32[1,2,16,64,1024]{4,3,2,1,0:T(8,128)}) fusion(bf16[2,2,16,64,1024]{4,3,2,1,0:T(8,128)(2,1)} %param.9), kind=kLoop, calls=%fused_computation.18 | loop fusion | flops 4194304 | bytes 25165824 | tf_op jit(solution)/shard_map/convert_element_type | solution.py:71
  53.5 8.4 %fusion.24 = (f32[1,1,16,64,1024]{4,3,2,1,0:T(8,128)}, f32[1,1,16,64,1024]{4,3,2,1,0:T(8,128)}) fusion(f32[1,2,16,64,1024]{4,3,2,1,0:T(8,128)} %get-tuple-element.20), kind=kLoop, calls=%fused_computation.59 | loop fusion | bytes 16777216 | tf_op jit(solution)/shard_map/slice | solution.py:72
  63.0 7.5 %all-to-all-start.3 = ((bf16[16,64,384]{2,1,0:T(8,128)(2,1)}), bf16[16,64,384]{2,1,0:T(8,128)(2,1)S(1)}, u32[]{:S(2)}, u32[]{:S(2)}) async-start(bf16[16,64,384]{2,1,0:T(8,128)(2,1)} %broadcast_in_dim.11), calls=%async_computation.3 | async-start | bytes 1572864 | tf_op jit(solution)/shard_map/all_to_all | solution.py:11
  70.7 8.4 %fusion.23 = (f32[1,1,16,64,1024]{4,3,2,1,0:T(8,128)}, f32[1,1,16,64,1024]{4,3,2,1,0:T(8,128)}) fusion(f32[1,2,16,64,1024]{4,3,2,1,0:T(8,128)} %get-tuple-element.19), kind=kLoop, calls=%fused_computation.58 | loop fusion | bytes 16777216 | tf_op jit(solution)/shard_map/slice | solution.py:72
  80.6 9.2 %all-to-all-done.3 = bf16[16,64,384]{2,1,0:T(8,128)(2,1)S(1)} async-done(((bf16[16,64,384]{2,1,0:T(8,128)(2,1)}), bf16[16,64,384]{2,1,0:T(8,128)(2,1)S(1)}, u32[]{:S(2)}, u32[]{:S(2)}) %all-to-all-start.3) | async-done | bytes 786464 | tf_op jit(solution)/shard_map/all_to_all | solution.py:11
  90.8 5.3 %all-to-all-start.1 = ((bf16[16,64,384]{2,1,0:T(8,128)(2,1)}), bf16[16,64,384]{2,1,0:T(8,128)(2,1)S(1)}, u32[]{:S(2)}, u32[]{:S(2)}) async-start(bf16[16,64,384]{2,1,0:T(8,128)(2,1)} %broadcast_in_dim.10), calls=%async_computation.1 | async-start | bytes 1572864 | tf_op jit(solution)/shard_map/all_to_all | solution.py:11
  96.3 1.4 fusion.13
  99.8 1.8 fusion.3
  104.8 3.4 %copy.35 = bf16[1,16,64,2,192]{2,1,3,0,4:T(8,128)(2,1)} copy(bf16[1,16,64,2,192]{4,3,2,1,0:T(2,128)(2,1)S(1)} %stack_reshape.7) | data formatting | bytes 1572864 | tf_op jit(solution)/shard_map/stack;reshape | solution.py:79
  108.2 6.8 %all-to-all-done.1 = bf16[16,64,384]{2,1,0:T(8,128)(2,1)S(1)} async-done(((bf16[16,64,384]{2,1,0:T(8,128)(2,1)}), bf16[16,64,384]{2,1,0:T(8,128)(2,1)S(1)}, u32[]{:S(2)}, u32[]{:S(2)}) %all-to-all-start.1) | async-done | bytes 786464 | tf_op jit(solution)/shard_map/all_to_all | solution.py:11
  115.3 1.4 fusion.9
  118.7 1.8 fusion.7
  121.9 1.3 add_convert_fusion.1
  123.8 3.4 %copy.34 = bf16[1,16,64,2,192]{2,1,3,0,4:T(8,128)(2,1)} copy(bf16[1,16,64,2,192]{4,3,2,1,0:T(2,128)(2,1)S(1)} %stack_reshape.6) | data formatting | bytes 1572864 | tf_op jit(solution)/shard_map/stack;reshape | solution.py:79
  127.2 2.5 %fusion.27 = bf16[192,2,2,16,64]{4,3,2,1,0:T(8,128)(2,1)S(1)} fusion(bf16[1,16,64,2,192]{2,1,3,0,4:T(8,128)(2,1)} %copy.35, bf16[1,16,64,2,192]{2,1,3,0,4:T(8,128)(2,1)} %copy.34), kind=kLoop, calls=%fused_computation.62 | loop fusion | flops 786432 | bytes 3145728
  129.7 3.3 %reshape.76 = bf16[16,2,24576]{2,1,0:T(2,128)(2,1)} reshape(bf16[192,2,2,16,64]{4,3,2,1,0:T(8,128)(2,1)S(1)} %fusion.27) | data formatting | bytes 3145728
  132.9 42.4 %all_to_all.45 = bf16[16,2,24576]{2,1,0:T(2,128)(2,1)} all-to-all(bf16[16,2,24576]{2,1,0:T(2,128)(2,1)} %reshape.76), channel_id=1, replica_groups=mesh['kgrp'=16,'wrow'=16] {'wrow'}, dimensions={0} | all-to-all | bytes 3145728 | tf_op jit(solution)/shard_map/all_to_all | solution.py:79
  175.3 3.8 %reshape.77 = bf16[192,2,2,16,64]{4,3,2,1,0:T(8,128)(2,1)S(1)} reshape(bf16[16,2,24576]{2,1,0:T(2,128)(2,1)} %all_to_all.45) | data formatting | bytes 3145728
  179.1 3.9 %copy.36 = bf16[2,16,64,2,192]{4,2,3,1,0:T(8,128)(2,1)} copy(bf16[2,16,64,2,192]{2,1,3,0,4:T(8,128)(2,1)S(1)} %bitcast.93) | data formatting | bytes 3145728 | tf_op jit(solution)/shard_map/all_to_all | solution.py:79
  183.0 2.0 convert_reduce_fusion
  185.0 1.4 copy.38
  187.3 1.5 copy.40
  188.8 3.1 %reshape.78 = f32[16,1,4608]{2,1,0:T(1,128)S(1)} reshape(f32[192,12,2,16]{3,2,1,0:T(2,128)S(1)} %bitcast.99) | data formatting | bytes 589824
  192.0 14.5 %all_to_all.46 = f32[16,1,4608]{2,1,0:T(1,128)S(1)} all-to-all(f32[16,1,4608]{2,1,0:T(1,128)S(1)} %reshape.78), channel_id=1, replica_groups=mesh['kgrp'=16,'wrow'=16] {'wrow'}, dimensions={0} | all-to-all | bytes 589824 | tf_op jit(solution)/shard_map/all_to_all | solution.py:86
  208.3 4.5 %reshape.79 = f32[192,12,2,16]{3,2,1,0:T(2,128)} reshape(f32[16,4608]{1,0:T(8,128)S(1)} %reduce.3) | data formatting | bytes 589824
  212.9 4.7 %copy.46 = f32[16,16,12,2,12]{4,1,3,0,2:T(8,128)S(1)} copy(f32[16,16,12,2,12]{0,3,4,2,1:T(2,128)} %bitcast.100) | data formatting | bytes 589824 | tf_op jit(solution)/shard_map/all_to_all | solution.py:86
  217.6 3.4 %broadcast_in_dim_reshape.3 = f32[1,16,12,384]{3,1,2,0:T(8,128)} reshape(f32[16,12,2,16,12]{4,3,2,0,1:T(8,128)S(1)} %bitcast.94) | data formatting | bytes 589824 | tf_op jit(solution)/shard_map/broadcast_in_dim;reshape | solution.py:88
  (50 shorter events, 17.4 us)
Async XLA Ops:
  0.0 13.3 %copy-start.12 = (s32[2]{0:T(128)S(1)}, s32[2]{0:T(128)}, u32[]{:S(2)}) copy-start(s32[2]{0:T(128)} %param.8) | copy-start | bytes 28
  1.9 28.8 %all-to-all-start = ((bf16[16,64,384]{2,1,0:T(8,128)(2,1)}), bf16[16,64,384]{2,1,0:T(8,128)(2,1)S(1)}, u32[]{:S(2)}, u32[]{:S(2)}) async-start(bf16[16,64,384]{2,1,0:T(8,128)(2,1)} %broadcast_in_dim.9), calls=%async_computation | async-start | bytes 1572864 | tf_op jit(solution)/shard_map/all_to_all | solution.py:11
  30.7 31.3 %all-to-all-start.2 = ((bf16[16,64,384]{2,1,0:T(8,128)(2,1)}), bf16[16,64,384]{2,1,0:T(8,128)(2,1)S(1)}, u32[]{:S(2)}, u32[]{:S(2)}) async-start(bf16[16,64,384]{2,1,0:T(8,128)(2,1)} %broadcast_in_dim.9), calls=%async_computation.2 | async-start | bytes 1572864 | tf_op jit(solution)/shard_map/all_to_all | solution.py:11
  61.9 17.5 %copy-start.4 = (bf16[16,64,384]{2,1,0:T(8,128)(2,1)}, bf16[16,64,384]{2,1,0:T(8,128)(2,1)S(1)}, u32[]{:S(2)}) copy-start(bf16[16,64,384]{2,1,0:T(8,128)(2,1)S(1)} %all-to-all-done.2) | copy-start | bytes 2359300
  63.0 26.7 %all-to-all-start.3 = ((bf16[16,64,384]{2,1,0:T(8,128)(2,1)}), bf16[16,64,384]{2,1,0:T(8,128)(2,1)S(1)}, u32[]{:S(2)}, u32[]{:S(2)}) async-start(bf16[16,64,384]{2,1,0:T(8,128)(2,1)} %broadcast_in_dim.11), calls=%async_computation.3 | async-start | bytes 1572864 | tf_op jit(solution)/shard_map/all_to_all | solution.py:11
  90.8 24.3 %all-to-all-start.1 = ((bf16[16,64,384]{2,1,0:T(8,128)(2,1)}), bf16[16,64,384]{2,1,0:T(8,128)(2,1)S(1)}, u32[]{:S(2)}, u32[]{:S(2)}) async-start(bf16[16,64,384]{2,1,0:T(8,128)(2,1)} %broadcast_in_dim.10), calls=%async_computation.1 | async-start | bytes 1572864 | tf_op jit(solution)/shard_map/all_to_all | solution.py:11
  96.3 2.2 copy-start
  96.3 3.5 %copy-start.1 = (f32[1,1,16,64,1024]{4,3,2,1,0:T(8,128)S(1)}, f32[1,1,16,64,1024]{4,3,2,1,0:T(8,128)}, u32[]{:S(2)}) copy-start(f32[1,1,16,64,1024]{4,3,2,1,0:T(8,128)} %get-tuple-element.22) | copy-start | bytes 12582916
  99.8 1.8 copy-start.5
  101.6 1.3 copy-start.8
  101.6 1.3 copy-start.10
  115.3 2.2 copy-start.2
  115.3 3.5 %copy-start.3 = (f32[1,1,16,64,1024]{4,3,2,1,0:T(8,128)S(1)}, f32[1,1,16,64,1024]{4,3,2,1,0:T(8,128)}, u32[]{:S(2)}) copy-start(f32[1,1,16,64,1024]{4,3,2,1,0:T(8,128)} %get-tuple-element.18) | copy-start | bytes 12582916
  118.7 1.8 copy-start.6
  120.6 1.3 copy-start.9
  120.6 1.3 copy-start.11
  185.0 1.4 copy-start.7
where the time goes:
time: 223 us; the launch traced here: 221 us
  local copies, waits for them, and re-layouts  65 us (29%)
  blocking collectives  56.9 us (26%)
  starting transfers between devices  35.7 us (16%)
  waiting for transfers between devices  21.7 us (10%)
  other arithmetic  20.4 us (9%)
  matrix products  12.2 us (5%)
  between operations  9.22 us (4%)
    all_to_all x1, blocking collectives, shards(): lax.all_to_all(jnp.stack(halves), 'wrow', split_axis=4, concat_axis=2, ti...  42.4 us
    all_to_all x4, starting transfers between devices, from_everyone(): lax.all_to_all(jnp.broadcast_to(array[None], (devices, *array.shape)), ax...  35.7 us
    all_to_all x4, waiting for transfers between devices, from_everyone(): lax.all_to_all(jnp.broadcast_to(array[None], (devices, *array.shape)), ax...  21.7 us
    unnamed x30, local copies, waits for them, and re-layouts  18.9 us
    slice x2, local copies, waits for them, and re-layouts, shards(): w_slice[0]  16.8 us
    all_to_all x1, blocking collectives, shards(): lax.all_to_all(column_block, 'wrow', split_axis=1, concat_axis=3, tiled=T...  14.5 us
    convert_element_type x1, other arithmetic, shards(): screened_w[q_slot].reshape(2, -1, screened_w.shape[-1]).astype(jnp.float32)  11.4 us
    another operation x4, local copies, waits for them, and re-layouts, shards(): jnp.stack(halves)  7.89 us
  transfers between devices with their start and end apart: 4, of which 3 were waited for; matrix products, arithmetic and copies ran while one was open for 19% of the time, Pallas kernels for 0%

commit v1 on v0

v1 whole, which is shorter than its diff:
```python
import functools

import jax
import jax.numpy as jnp
from jax import lax
from jax.experimental import pallas as pl
from jax.experimental.pallas import tpu as pltpu
from jax.sharding import PartitionSpec as P

BETA = 8.0
MESH = pl.DeviceIdType.MESH
NT = (((1,), (1,)), ((), ()))
NN = (((1,), (0,)), ((), ()))


def sign_row(width, first, second):
    half = width // 2
    lane = lax.broadcasted_iota(jnp.int32, (1, width), 1)
    return jnp.where(lane < half, first, second).astype(jnp.float32)


def swap_halves(x):
    half = x.shape[1] // 2
    return jnp.concatenate([x[:, half:], x[:, :half]], axis=1)


def kernel(perm_ref, mom_ref, energy_ref, orb_ref, w_hbm, out_ref,
           xs, kg, wv, scr, lsc, hsend, hrecv, xkt, order, occ,
           rsend, rrecv, fsend, frecv,
           gsend, grecv, ksend, krecv, kcore, hss, hrs, rss, rrs, fss, frs, wsem, osem):
    g = lax.axis_index("kgrp")
    w = lax.axis_index("wrow")
    y, h, c = lax.div(g, 4), lax.rem(lax.div(g, 2), 2), lax.rem(g, 2)
    z, x = lax.div(w, 4), lax.rem(w, 4)
    rows, width = xs.shape[2], xs.shape[3]
    taus = wv.shape[2]

    def wrap(v):
        return lax.rem(v, 4)

    def kdev(y_, h_, c_):
        return y_ * 4 + h_ * 2 + c_

    def wdev(z_, x_):
        return z_ * 4 + x_

    own_x = pltpu.make_async_copy(orb_ref.at[0], xs.at[0, w], osem.at[0])
    own_k = pltpu.make_async_copy(orb_ref.at[0], kg.at[g], osem.at[1])
    own_x.start()
    own_k.start()

    barrier = pltpu.get_barrier_semaphore()
    partner = kdev(y, h, 1 - c)
    across = kdev(y, 1 - h, c)
    up, down = kdev(wrap(y + 1), h, c), kdev(wrap(y + 3), h, c)
    beyond = kdev(wrap(y + 2), h, c)
    for peer in (across, up, down, beyond, partner):
        pl.semaphore_signal(barrier, inc=1, device_id=(peer, w), device_id_type=MESH)
    for d in (2, 1, 3):
        pl.semaphore_signal(barrier, inc=1, device_id=(g, wdev(wrap(z + d), x)), device_id_type=MESH)
        pl.semaphore_signal(barrier, inc=1, device_id=(g, wdev(z, wrap(x + d))), device_id_type=MESH)
    own_x.wait()
    own_k.wait()
    pl.semaphore_wait(barrier, 11)

    def kcopy(block, peer):
        return pltpu.make_async_remote_copy(
            src_ref=kg.at[block], dst_ref=kg.at[block], send_sem=ksend.at[0],
            recv_sem=krecv.at[block], device_id=(peer, w), device_id_type=MESH)

    def kpass(block):
        pltpu.make_async_remote_copy(
            src_ref=kg.at[block], dst_ref=kg.at[block], send_sem=ksend.at[0],
            recv_sem=kcore.at[0], device_id=(partner, w), device_id_type=MESH).start()

    def kwait(block):
        kcopy(block, across).wait_recv()

    def gcopy(s, block, peer):
        return pltpu.make_async_remote_copy(
            src_ref=xs.at[s, block], dst_ref=xs.at[s, block], send_sem=gsend.at[s],
            recv_sem=grecv.at[s, block], device_id=(g, peer), device_id_type=MESH)

    left, right = wdev(z, wrap(x + 3)), wdev(z, wrap(x + 1))

    def gwait(s, block):
        gcopy(s, block, right).wait_recv()

    def gstart_z(s):
        gcopy(s, w, wdev(wrap(z + 1), x)).start()
        gcopy(s, w, wdev(wrap(z + 3), x)).start()
        gcopy(s, w, wdev(wrap(z + 2), x)).start()

    def gstart_x(s):
        gcopy(s, w, right).start()
        gcopy(s, w, left).start()

    def gforward(s, d):
        block = wdev(wrap(z + d), x)
        gwait(s, block)
        gcopy(s, block, right).start()
        gcopy(s, block, left).start()

    def grelay(s, d):
        if d < 2:
            block, peer = wdev(wrap(z + d), wrap(x + 3)), right
        else:
            block, peer = wdev(wrap(z + d), wrap(x + 1)), left
        gwait(s, block)
        gcopy(s, block, peer).start()

    def gfinish(s, d):
        gwait(s, wdev(wrap(z + d), wrap(x + (1 if d < 2 else 3))))
        gwait(s, wdev(wrap(z + d), wrap(x + 2)))

    def kspread(block):
        for peer in (beyond, up, down):
            kcopy(block, peer).start()

    def ktake(yy, hh):
        block = kdev(wrap(y + yy), hh, c)
        kwait(block)
        kpass(block)

    kcopy(g, across).start()
    kspread(g)
    gstart_x(0)
    kpass(g)
    for i in range(4):
        pltpu.make_async_copy(w_hbm.at[i // 2, i % 2], wv.at[i // 2, i % 2], wsem.at[i]).start()
    ktake(1, h)
    gstart_z(0)
    ktake(3, h)
    ktake(2, h)
    grelay(0, 0)
    row = lax.broadcasted_iota(jnp.int32, (192, 192), 0)
    col = lax.broadcasted_iota(jnp.int32, (192, 192), 1)
    part, inner = lax.div(row, 48), lax.rem(row, 48)
    split = lax.div(inner, 12) * 48 + part * 12 + lax.rem(inner, 12)
    tau_row = lax.rem(row, 16)
    merge = lax.rem(tau_row, 4) * 48 + lax.div(tau_row, 4) * 12 + lax.div(row, 16)
    order[0] = jnp.where(col == split, 1.0, 0.0).astype(jnp.bfloat16)
    order[1] = jnp.where(col == merge, 1.0, 0.0).astype(jnp.bfloat16)
    own_row = perm_ref[pl.ds(g, 1), :]
    lane = lax.broadcasted_iota(jnp.int32, own_row.shape, 1)
    sources = [jnp.sum(jnp.where(lane == mom_ref[q], own_row, 0)) for q in range(2)]
    gfinish(0, 0)
    row = lax.broadcasted_iota(jnp.int32, (width, width), 0)
    col = lax.broadcasted_iota(jnp.int32, (width, width), 1)
    pick = jnp.where(row == col, 1.0, 0.0).astype(jnp.bfloat16)
    strip = xs[0, pl.ds(z * 4, 4)].reshape(4 * rows, width)
    xkt[...] = lax.dot_general(pick, strip, NT, preferred_element_type=jnp.float32).astype(jnp.bfloat16)
    mine = kdev(y, 1 - h, c)
    kwait(mine)
    kspread(mine)
    kpass(mine)
    gforward(0, 1)
    gforward(0, 3)
    gforward(0, 2)
    ktake(1, 1 - h)
    ktake(3, 1 - h)
    ktake(2, 1 - h)
    grelay(0, 1)
    grelay(0, 3)
    pltpu.make_async_remote_copy(
        src_ref=kg.at[pl.ds(0, 8)], dst_ref=kg.at[pl.ds(0, 8)], send_sem=ksend.at[0],
        recv_sem=kcore.at[0], device_id=(partner, w), device_id_type=MESH).wait_recv()

    for q in range(2):
        xs[1 + q, w] = kg[sources[q]]
    for s in (1, 2):
        gstart_z(s)
        gstart_x(s)

    minus_plus = sign_row(width, -1.0, 1.0)
    plus_minus = sign_row(width, 1.0, -1.0)
    tau = (lax.broadcasted_iota(jnp.int32, (taus, 1), 0).astype(jnp.float32) + 0.5) * (BETA / taus)
    for q in range(2):
        energy = energy_ref[pl.ds(sources[q], 1), :]
        soft = -BETA * energy
        soft = jnp.maximum(soft, 0.0) + jnp.log(1.0 + jnp.exp(-jnp.abs(soft)))
        factor = -jnp.exp(-tau * energy - soft)
        occ[q] = jnp.concatenate([factor, factor], axis=1)

    def tau_of(r, e):
        return r * 4 + wrap(x + e)

    def left_rows(q, r):
        base = xs[1 + q, w].astype(jnp.float32)
        scaled = jnp.concatenate(
            [base * occ[q, pl.ds(tau_of(r, e), 1), :] for e in range(4)], axis=0)
        lsc[q, r, :256] = scaled.astype(jnp.bfloat16)
        lsc[q, r, 256:] = (swap_halves(scaled) * plus_minus).astype(jnp.bfloat16)

    def left_round(r, carry):
        left_rows(0, r)
        left_rows(1, r)
        return carry

    lax.fori_loop(0, 4, left_round, 0, unroll=True)
    grelay(0, 2)

    def screen(q, n, r):
        cols = pl.ds(pl.multiple_of(n * 256, 256), 256)
        tile = xs[1 + q, pl.ds(n * 4, 4)].reshape(256, width)
        green = lax.dot_general(lsc[q, r], tile, NT, preferred_element_type=jnp.float32)
        for e in range(4):
            t = tau_of(r, e)
            real_rows, imag_rows = slice(e * 64, e * 64 + 64), slice(256 + e * 64, 320 + e * 64)
            gr, gi = green[real_rows], green[imag_rows]
            wr = wv[q, 0, t, :, cols].astype(jnp.float32)
            wi = wv[q, 1, t, :, cols].astype(jnp.float32)
            sr = gr * wr - gi * wi
            si = gr * wi + gi * wr
            if q == 1:
                sr = sr + scr[r, real_rows, cols].astype(jnp.float32)
                si = si + scr[r, imag_rows, cols].astype(jnp.float32)
            scr[r, real_rows, cols] = sr.astype(jnp.bfloat16)
            scr[r, imag_rows, cols] = si.astype(jnp.bfloat16)

    def tile(q, d):
        n = wrap(z + d)

        def one_round(r, carry):
            screen(q, n, r)
            return carry

        lax.fori_loop(0, 4, one_round, 0, unroll=True)

    grelay(1, 0)
    gforward(1, 1)
    gforward(1, 3)
    gforward(1, 2)
    for d in (1, 3, 2):
        gfinish(0, d)
    for i in range(2):
        pltpu.make_async_copy(w_hbm.at[0, i], wv.at[0, i], wsem.at[i]).wait()
    gfinish(1, 0)
    tile(0, 0)
    grelay(1, 1)
    grelay(1, 3)
    gforward(2, 1)
    grelay(2, 0)
    gfinish(1, 1)
    tile(0, 1)
    gforward(2, 3)
    grelay(1, 2)
    gforward(2, 2)
    gfinish(1, 3)
    tile(0, 3)
    grelay(2, 1)
    grelay(2, 3)
    gfinish(1, 2)
    tile(0, 2)
    for i in range(2):
        pltpu.make_async_copy(w_hbm.at[1, i], wv.at[1, i], wsem.at[2 + i]).wait()
    gfinish(2, 0)
    tile(1, 0)
    grelay(2, 2)
    gfinish(2, 1)
    tile(1, 1)
    gfinish(2, 3)
    tile(1, 3)
    gfinish(2, 2)

    def hcopy(r, e):
        return pltpu.make_async_remote_copy(
            src_ref=hsend.at[r, e], dst_ref=hrecv.at[r, x], send_sem=hss.at[0],
            recv_sem=hrs.at[r], device_id=(g, wdev(z, wrap(x + e))), device_id_type=MESH)

    def last(r, carry):
        screen(1, wrap(z + 2), r)
        both = lax.dot_general(scr[r], xs[0].reshape(16 * rows, width), NN,
                               preferred_element_type=jnp.float32)
        half = both[:256] + swap_halves(both[256:]) * minus_plus
        half = half.astype(jnp.bfloat16)
        for e in (2, 1, 3):
            hsend[r, e] = half[e * 64:e * 64 + 64]
        hrecv[r, x] = half[:64]
        for e in (2, 1, 3):
            hcopy(r, e).start()
        return carry

    lax.fori_loop(0, 4, last, 0, unroll=True)

    def rcopy(r, d):
        other = wrap(z + d)
        return pltpu.make_async_remote_copy(
            src_ref=rsend.at[r, other], dst_ref=rrecv.at[r, z], send_sem=rss.at[0],
            recv_sem=rrs.at[0], device_id=(g, wdev(other, x)), device_id_type=MESH)

    def project(r):
        pltpu.make_async_remote_copy(
            src_ref=hrecv.at[r, pl.ds(0, 3)], dst_ref=hrecv.at[r, pl.ds(0, 3)], send_sem=hss.at[0],
            recv_sem=hrs.at[r], device_id=(g, right), device_id_type=MESH).wait_recv()
        total = lax.dot_general(xkt[...], hrecv[r].reshape(4 * rows, width), NN,
                                preferred_element_type=jnp.float32)
        sigma = total[:192] + swap_halves(total[192:]) * plus_minus
        sigma = sigma.reshape(4, 48, width)
        rsend[r] = sigma.astype(jnp.bfloat16)
        for d in (2, 1, 3):
            rcopy(r, d).start()

    for r in range(4):
        project(r)

    pltpu.make_async_remote_copy(
        src_ref=rrecv.at[pl.ds(0, 3)], dst_ref=rrecv.at[pl.ds(0, 3)], send_sem=rss.at[0],
        recv_sem=rrs.at[0], device_id=(g, right), device_id_type=MESH).wait_recv()
    sums = []
    for r in range(4):
        total = rsend[r, z].astype(jnp.float32)
        for d in range(1, 4):
            total = total + rrecv[r, wrap(z + d)].astype(jnp.float32)
        sums.append(total)
    summed = jnp.concatenate(sums, axis=0).astype(jnp.bfloat16)
    pieces = lax.dot_general(order[0], summed, NN, preferred_element_type=jnp.float32)
    fsend[...] = pieces.astype(jnp.bfloat16).reshape(4, 48, width)
    frecv[x] = fsend[x]
    for e in (2, 1, 3):
        other = wrap(x + e)
        pltpu.make_async_remote_copy(
            src_ref=fsend.at[other], dst_ref=frecv.at[x], send_sem=fss.at[0],
            recv_sem=frs.at[0], device_id=(g, wdev(z, other)), device_id_type=MESH).start()

    for s in range(3):
        pltpu.make_async_remote_copy(
            src_ref=xs.at[s, pl.ds(0, 15)], dst_ref=xs.at[s, pl.ds(0, 15)], send_sem=gsend.at[s],
            recv_sem=grecv.at[s, 0], device_id=(g, right), device_id_type=MESH).wait_send()
    pltpu.make_async_remote_copy(
        src_ref=kg.at[pl.ds(0, 15)], dst_ref=kg.at[pl.ds(0, 15)], send_sem=ksend.at[0],
        recv_sem=kcore.at[0], device_id=(partner, w), device_id_type=MESH).wait_send()
    pltpu.make_async_remote_copy(
        src_ref=hsend.at[pl.ds(0, 3)], dst_ref=hrecv.at[pl.ds(0, 3)], send_sem=hss.at[0],
        recv_sem=hrs.at[0], device_id=(g, right), device_id_type=MESH).wait_send()
    pltpu.make_async_remote_copy(
        src_ref=rsend.at[pl.ds(0, 3)], dst_ref=rrecv.at[pl.ds(0, 3)], send_sem=rss.at[0],
        recv_sem=rrs.at[0], device_id=(g, right), device_id_type=MESH).wait_send()
    pltpu.make_async_remote_copy(
        src_ref=fsend.at[pl.ds(0, 3)], dst_ref=frecv.at[pl.ds(0, 3)], send_sem=fss.at[0],
        recv_sem=frs.at[0], device_id=(g, right), device_id_type=MESH).wait()
    out_ref[0] = lax.dot_general(order[1], frecv[...].reshape(192, width), NN,
                                 preferred_element_type=jnp.float32).reshape(12, 16, width)


def shards(orbitals, energies, perm_table, momenta, screened_w):
    _, rows, width = orbitals.shape
    taus, points = screened_w.shape[2], screened_w.shape[4]
    bf16, f32 = jnp.bfloat16, jnp.float32
    dma = pltpu.SemaphoreType.DMA
    smem = pl.BlockSpec(memory_space=pltpu.SMEM)
    vmem = pl.BlockSpec(memory_space=pltpu.VMEM)
    sigma = pl.pallas_call(
        kernel,
        out_shape=jax.ShapeDtypeStruct((1, 12, taus, width), f32),
        in_specs=[vmem, smem, vmem, pl.BlockSpec(memory_space=pl.ANY), pl.BlockSpec(memory_space=pl.ANY)],
        out_specs=vmem,
        scratch_shapes=[
            pltpu.VMEM((3, 16, rows, width), bf16),
            pltpu.VMEM((16, rows, width), bf16),
            pltpu.VMEM((2, 2, taus, rows, points), bf16),
            pltpu.VMEM((4, 512, points), bf16),
            pltpu.VMEM((2, 4, 512, width), bf16),
            pltpu.VMEM((4, 4, rows, width), bf16),
            pltpu.VMEM((4, 4, rows, width), bf16),
            pltpu.VMEM((width, 4 * rows), bf16),
            pltpu.VMEM((2, 192, 192), bf16),
            pltpu.VMEM((2, taus, width), f32),
            pltpu.VMEM((4, 4, 48, width), bf16),
            pltpu.VMEM((4, 4, 48, width), bf16),
            pltpu.VMEM((4, 48, width), bf16),
            pltpu.VMEM((4, 48, width), bf16),
            dma((3,)), dma((3, 16)), dma((1,)), dma((16,)), dma((1,)),
            dma((1,)), dma((4,)), dma((1,)), dma((1,)), dma((1,)), dma((1,)),
            dma((4,)), dma((2,)),
        ],
        compiler_params=pltpu.CompilerParams(collective_id=0, has_side_effects=True),
    )(perm_table.T, momenta, energies, orbitals, screened_w)
    return sigma.transpose(0, 2, 1, 3)


def solution(mesh):
    return jax.shard_map(
        shards,
        mesh=mesh,
        in_specs=(P("kgrp", "wrow", None), P(), P(), P(), P(None, None, None, "wrow", None)),
        out_specs=P("kgrp", None, "wrow", None),
        check_vma=False,
    )
```

time: 223 us -> 71.9 us (0.32)
  Pallas kernels: 0 us -> 69.7 us
  local copies, waits for them, and re-layouts: 65 us -> 1.69 us
  blocking collectives: 56.9 us -> 0 us
  starting transfers between devices: 35.7 us -> 0 us
  waiting for transfers between devices: 21.7 us -> 0 us
  other arithmetic: 20.4 us -> 0 us
  matrix products: 12.2 us -> 0 us
  between operations: 9.22 us -> 0.01 us
    pallas_call x0 -> x1, Pallas kernels: none -> 69.7 us  [shards(): pl.pallas_call(kernel, out_shape=jax.ShapeDtypeStruct((1, 12, taus, width...]
    all_to_all x2 -> x0, blocking collectives: 56.9 us -> none  [the longest x1 42.4 us: shards(): lax.all_to_all(jnp.stack(halves), 'wrow', split_axis=4, concat_axis=2, ti...]
    all_to_all x4 -> x0, starting transfers between devices: 35.7 us -> none  [from_everyone(): lax.all_to_all(jnp.broadcast_to(array[None], (devices, *array.shape)), ax...]
    all_to_all x4 -> x0, waiting for transfers between devices: 21.7 us -> none  [from_everyone(): lax.all_to_all(jnp.broadcast_to(array[None], (devices, *array.shape)), ax...]
    slice x3 -> x0, local copies, waits for them, and re-layouts: 17.4 us -> none  [the longest x2 16.8 us: shards(): w_slice[0]]
    unnamed x30 -> x1, local copies, waits for them, and re-layouts: 18.9 us -> 1.69 us
    another operation x6 -> x0, local copies, waits for them, and re-layouts: 12.8 us -> none  [the longest x4 7.89 us: shards(): jnp.stack(halves)]
    dot_general x9 -> x0, matrix products: 12.2 us -> none  [the longest x2 3.66 us: shards(): jnp.dot(flat_left, columns_shard_piece.T, preferred_element_type=jnp.floa...]
  transfers between devices with their start and end apart: 4 -> 0, of which waited for: 3 -> 0; matrix products, arithmetic and copies ran while one was open for 19% -> 0% of each run, Pallas kernels for 0% -> 0%
where the time goes in v1:
time: 71.9 us; the launch traced here: 71.4 us
  Pallas kernels  69.7 us (97%)
  local copies, waits for them, and re-layouts  1.69 us (2%)
    pallas_call x1, Pallas kernels, shards(): pl.pallas_call(kernel, out_shape=jax.ShapeDtypeStruct((1, 12, taus, width...  69.7 us
    unnamed x1, local copies, waits for them, and re-layouts  1.69 us

profile of v1, /device:TPU:16, one launch (start us, length us, event | category | flops | bytes accessed | tf_op | source)
XLA Modules:
  0.0 71.4 jit_solution(6935546161643872838)
XLA Ops:
  0.0 69.7 %shard_map.55 = f32[1,12,16,384]{3,2,1,0:T(8,128)} custom-call(s32[16,64]{1,0:T(8,128)} %bitcast.3, s32[2]{0:T(128)} %mom_ref.1, f32[16,192]{1,0:T(8,128)} %energy_ref.1, bf16[1,64,384]{2,1,0:T(8,128)(2,1)} %orb_ref.1, bf16[2,2,16,64,1024]{4,3,2,1,0:T(8,128)(2,1)} %w_hbm.1), custom_call_target="tpu_custom_call" | custom-call | tf_op jit(solution)/shard_map/pallas_call | solution.py:353
  69.7 1.7 %copy.7 = f32[1,16,12,384]{3,1,2,0:T(8,128)} copy(f32[1,16,12,384]{3,1,2,0:T(8,128)} %bitcast.2) | data formatting | bytes 589824

commit v2 on v1

--- a/solution.py
+++ b/solution.py
@@ -144,12 +144,6 @@
     own_row = perm_ref[pl.ds(g, 1), :]
     lane = lax.broadcasted_iota(jnp.int32, own_row.shape, 1)
     sources = [jnp.sum(jnp.where(lane == mom_ref[q], own_row, 0)) for q in range(2)]
-    gfinish(0, 0)
-    row = lax.broadcasted_iota(jnp.int32, (width, width), 0)
-    col = lax.broadcasted_iota(jnp.int32, (width, width), 1)
-    pick = jnp.where(row == col, 1.0, 0.0).astype(jnp.bfloat16)
-    strip = xs[0, pl.ds(z * 4, 4)].reshape(4 * rows, width)
-    xkt[...] = lax.dot_general(pick, strip, NT, preferred_element_type=jnp.float32).astype(jnp.bfloat16)
     mine = kdev(y, 1 - h, c)
     kwait(mine)
     kspread(mine)
@@ -157,6 +151,12 @@
     gforward(0, 1)
     gforward(0, 3)
     gforward(0, 2)
+    gfinish(0, 0)
+    row = lax.broadcasted_iota(jnp.int32, (width, width), 0)
+    col = lax.broadcasted_iota(jnp.int32, (width, width), 1)
+    pick = jnp.where(row == col, 1.0, 0.0).astype(jnp.bfloat16)
+    strip = xs[0, pl.ds(z * 4, 4)].reshape(4 * rows, width)
+    xkt[...] = lax.dot_general(pick, strip, NT, preferred_element_type=jnp.float32).astype(jnp.bfloat16)
     ktake(1, 1 - h)
     ktake(3, 1 - h)
     ktake(2, 1 - h)
@@ -168,9 +168,9 @@
 
     for q in range(2):
         xs[1 + q, w] = kg[sources[q]]
-    for s in (1, 2):
-        gstart_z(s)
-        gstart_x(s)
+    gstart_z(1)
+    gstart_x(1)
+    gstart_x(2)
 
     minus_plus = sign_row(width, -1.0, 1.0)
     plus_minus = sign_row(width, 1.0, -1.0)
@@ -227,24 +227,23 @@
 
         lax.fori_loop(0, 4, one_round, 0, unroll=True)
 
+    gstart_z(2)
     grelay(1, 0)
     gforward(1, 1)
     gforward(1, 3)
+    grelay(2, 0)
     gforward(1, 2)
-    for d in (1, 3, 2):
-        gfinish(0, d)
     for i in range(2):
         pltpu.make_async_copy(w_hbm.at[0, i], wv.at[0, i], wsem.at[i]).wait()
+    grelay(1, 1)
+    grelay(1, 3)
     gfinish(1, 0)
     tile(0, 0)
-    grelay(1, 1)
-    grelay(1, 3)
     gforward(2, 1)
-    grelay(2, 0)
+    gforward(2, 3)
+    grelay(1, 2)
     gfinish(1, 1)
     tile(0, 1)
-    gforward(2, 3)
-    grelay(1, 2)
     gforward(2, 2)
     gfinish(1, 3)
     tile(0, 3)
@@ -262,6 +261,8 @@
     gfinish(2, 3)
     tile(1, 3)
     gfinish(2, 2)
+    for d in (1, 3, 2):
+        gfinish(0, d)
 
     def hcopy(r, e):
         return pltpu.make_async_remote_copy(

time: 71.9 us -> 66 us (0.918)
  Pallas kernels: 69.7 us -> 64.1 us
    pallas_call x1, Pallas kernels: 69.7 us -> 64.1 us  [shards(): pl.pallas_call(kernel, out_shape=jax.ShapeDtypeStruct((1, 12, taus, width...]
where the time goes in v2:
time: 66 us; the launch traced here: 65.8 us
  Pallas kernels  64.1 us (97%)
  local copies, waits for them, and re-layouts  1.69 us (3%)
    pallas_call x1, Pallas kernels, shards(): pl.pallas_call(kernel, out_shape=jax.ShapeDtypeStruct((1, 12, taus, width...  64.1 us
    unnamed x1, local copies, waits for them, and re-layouts  1.69 us

profile of v2, /device:TPU:16, one launch (start us, length us, event | category | flops | bytes accessed | tf_op | source)
XLA Modules:
  0.0 65.8 jit_solution(2496955919340478257)
XLA Ops:
  0.0 64.1 %shard_map.55 = f32[1,12,16,384]{3,2,1,0:T(8,128)} custom-call(s32[16,64]{1,0:T(8,128)} %bitcast.3, s32[2]{0:T(128)} %mom_ref.1, f32[16,192]{1,0:T(8,128)} %energy_ref.1, bf16[1,64,384]{2,1,0:T(8,128)(2,1)} %orb_ref.1, bf16[2,2,16,64,1024]{4,3,2,1,0:T(8,128)(2,1)} %w_hbm.1), custom_call_target="tpu_custom_call" | custom-call | tf_op jit(solution)/shard_map/pallas_call | solution.py:354
  64.1 1.7 %copy.7 = f32[1,16,12,384]{3,1,2,0:T(8,128)} copy(f32[1,16,12,384]{3,1,2,0:T(8,128)} %bitcast.2) | data formatting | bytes 589824

commit v3 on v2

--- a/solution.py
+++ b/solution.py
@@ -19,13 +19,20 @@
     return jnp.where(lane < half, first, second).astype(jnp.float32)
 
 
+def pack_columns(x):
+    return jnp.concatenate([x[:, :192], x[:, 320:], x[:, 192:320]], axis=1)
+
+
+def unpack_columns(x):
+    return jnp.concatenate([x[:, :192], x[:, 256:], x[:, 192:256]], axis=1)
+
+
 def swap_halves(x):
-    half = x.shape[1] // 2
-    return jnp.concatenate([x[:, half:], x[:, :half]], axis=1)
-
-
-def kernel(perm_ref, mom_ref, energy_ref, orb_ref, w_hbm, out_ref,
-           xs, kg, wv, scr, lsc, hsend, hrecv, xkt, order, occ,
+    return jnp.concatenate([x[:, 256:], pltpu.roll(x[:, 128:256], 64, axis=1), x[:, :128]], axis=1)
+
+
+def kernel(perm_hbm, mom_hbm, energy_hbm, orb_ref, w_hbm, out_ref,
+           perm_ref, mom_ref, energy_ref, own, xs, kg, wv, scr, lsc, hsend, hrecv, xkt, order, occ,
            rsend, rrecv, fsend, frecv,
            gsend, grecv, ksend, krecv, kcore, hss, hrs, rss, rrs, fss, frs, wsem, osem):
     g = lax.axis_index("kgrp")
@@ -44,10 +51,13 @@
     def wdev(z_, x_):
         return z_ * 4 + x_
 
-    own_x = pltpu.make_async_copy(orb_ref.at[0], xs.at[0, w], osem.at[0])
-    own_k = pltpu.make_async_copy(orb_ref.at[0], kg.at[g], osem.at[1])
-    own_x.start()
-    own_k.start()
+    own_rows = pltpu.make_async_copy(orb_ref.at[0], own, osem.at[0])
+    tables = [
+        pltpu.make_async_copy(src, dst, osem.at[1 + i])
+        for i, (src, dst) in enumerate(((perm_hbm, perm_ref), (mom_hbm, mom_ref), (energy_hbm, energy_ref)))]
+    own_rows.start()
+    for table in tables:
+        table.start()
 
     barrier = pltpu.get_barrier_semaphore()
     partner = kdev(y, h, 1 - c)
@@ -59,8 +69,10 @@
     for d in (2, 1, 3):
         pl.semaphore_signal(barrier, inc=1, device_id=(g, wdev(wrap(z + d), x)), device_id_type=MESH)
         pl.semaphore_signal(barrier, inc=1, device_id=(g, wdev(z, wrap(x + d))), device_id_type=MESH)
-    own_x.wait()
-    own_k.wait()
+    own_rows.wait()
+    packed = pack_columns(own[...])
+    xs[0, w] = packed
+    kg[g] = packed
     pl.semaphore_wait(barrier, 11)
 
     def kcopy(block, peer):
@@ -141,6 +153,8 @@
     merge = lax.rem(tau_row, 4) * 48 + lax.div(tau_row, 4) * 12 + lax.div(row, 16)
     order[0] = jnp.where(col == split, 1.0, 0.0).astype(jnp.bfloat16)
     order[1] = jnp.where(col == merge, 1.0, 0.0).astype(jnp.bfloat16)
+    for table in tables:
+        table.wait()
     own_row = perm_ref[pl.ds(g, 1), :]
     lane = lax.broadcasted_iota(jnp.int32, own_row.shape, 1)
     sources = [jnp.sum(jnp.where(lane == mom_ref[q], own_row, 0)) for q in range(2)]
@@ -154,7 +168,8 @@
     gfinish(0, 0)
     row = lax.broadcasted_iota(jnp.int32, (width, width), 0)
     col = lax.broadcasted_iota(jnp.int32, (width, width), 1)
-    pick = jnp.where(row == col, 1.0, 0.0).astype(jnp.bfloat16)
+    want = jnp.where(row < 192, row, 192 + lax.rem(row + 64, 192))
+    pick = jnp.where(want == col, 1.0, 0.0).astype(jnp.bfloat16)
     strip = xs[0, pl.ds(z * 4, 4)].reshape(4 * rows, width)
     xkt[...] = lax.dot_general(pick, strip, NT, preferred_element_type=jnp.float32).astype(jnp.bfloat16)
     ktake(1, 1 - h)
@@ -180,7 +195,7 @@
         soft = -BETA * energy
         soft = jnp.maximum(soft, 0.0) + jnp.log(1.0 + jnp.exp(-jnp.abs(soft)))
         factor = -jnp.exp(-tau * energy - soft)
-        occ[q] = jnp.concatenate([factor, factor], axis=1)
+        occ[q] = pack_columns(jnp.concatenate([factor, factor], axis=1))
 
     def tau_of(r, e):
         return r * 4 + wrap(x + e)
@@ -235,27 +250,27 @@
     gforward(1, 2)
     for i in range(2):
         pltpu.make_async_copy(w_hbm.at[0, i], wv.at[0, i], wsem.at[i]).wait()
+    gfinish(1, 0)
+    tile(0, 0)
     grelay(1, 1)
     grelay(1, 3)
-    gfinish(1, 0)
-    tile(0, 0)
     gforward(2, 1)
     gforward(2, 3)
+    gforward(2, 2)
     grelay(1, 2)
     gfinish(1, 1)
     tile(0, 1)
-    gforward(2, 2)
     gfinish(1, 3)
     tile(0, 3)
     grelay(2, 1)
     grelay(2, 3)
     gfinish(1, 2)
     tile(0, 2)
+    grelay(2, 2)
     for i in range(2):
         pltpu.make_async_copy(w_hbm.at[1, i], wv.at[1, i], wsem.at[2 + i]).wait()
     gfinish(2, 0)
     tile(1, 0)
-    grelay(2, 2)
     gfinish(2, 1)
     tile(1, 1)
     gfinish(2, 3)
@@ -340,8 +355,9 @@
     pltpu.make_async_remote_copy(
         src_ref=fsend.at[pl.ds(0, 3)], dst_ref=frecv.at[pl.ds(0, 3)], send_sem=fss.at[0],
         recv_sem=frs.at[0], device_id=(g, right), device_id_type=MESH).wait()
-    out_ref[0] = lax.dot_general(order[1], frecv[...].reshape(192, width), NN,
-                                 preferred_element_type=jnp.float32).reshape(12, 16, width)
+    result = lax.dot_general(order[1], frecv[...].reshape(192, width), NN,
+                             preferred_element_type=jnp.float32)
+    out_ref[0] = unpack_columns(result).reshape(12, 16, width)
 
 
 def shards(orbitals, energies, perm_table, momenta, screened_w):
@@ -349,14 +365,18 @@
     taus, points = screened_w.shape[2], screened_w.shape[4]
     bf16, f32 = jnp.bfloat16, jnp.float32
     dma = pltpu.SemaphoreType.DMA
-    smem = pl.BlockSpec(memory_space=pltpu.SMEM)
+    hbm = pl.BlockSpec(memory_space=pltpu.HBM)
     vmem = pl.BlockSpec(memory_space=pltpu.VMEM)
     sigma = pl.pallas_call(
         kernel,
         out_shape=jax.ShapeDtypeStruct((1, 12, taus, width), f32),
-        in_specs=[vmem, smem, vmem, pl.BlockSpec(memory_space=pl.ANY), pl.BlockSpec(memory_space=pl.ANY)],
+        in_specs=[hbm] * 5,
         out_specs=vmem,
         scratch_shapes=[
+            pltpu.VMEM(perm_table.shape[::-1], jnp.int32),
+            pltpu.SMEM(momenta.shape, jnp.int32),
+            pltpu.VMEM(energies.shape, f32),
+            pltpu.VMEM((rows, width), bf16),
             pltpu.VMEM((3, 16, rows, width), bf16),
             pltpu.VMEM((16, rows, width), bf16),
             pltpu.VMEM((2, 2, taus, rows, points), bf16),
@@ -373,10 +393,11 @@
             pltpu.VMEM((4, 48, width), bf16),
             dma((3,)), dma((3, 16)), dma((1,)), dma((16,)), dma((1,)),
             dma((1,)), dma((4,)), dma((1,)), dma((1,)), dma((1,)), dma((1,)),
-            dma((4,)), dma((2,)),
+            dma((4,)), dma((4,)),
         ],
-        compiler_params=pltpu.CompilerParams(collective_id=0, has_side_effects=True),
-    )(perm_table.T, momenta, energies, orbitals, screened_w)
+        compiler_params=pltpu.CompilerParams(collective_id=0, has_side_effects=True, vmem_limit_bytes=40 * 2**20),
+    )(*[pltpu.with_memory_space_constraint(a, pltpu.HBM)
+        for a in (perm_table.T, momenta, energies, orbitals, screened_w)])
     return sigma.transpose(0, 2, 1, 3)
 
 

time: 66 us -> 63 us (0.955)
  Pallas kernels: 64.1 us -> 62.1 us
  local copies, waits for them, and re-layouts: 1.69 us -> 0.72 us
    pallas_call x1, Pallas kernels: 64.1 us -> 62.1 us  [shards(): pl.pallas_call(kernel, out_shape=jax.ShapeDtypeStruct((1, 12, taus, width...]
    unnamed x1, local copies, waits for them, and re-layouts: 1.69 us -> 0.72 us
where the time goes in v3:
time: 63 us; the launch traced here: 62.8 us
  Pallas kernels  62.1 us (99%)
  local copies, waits for them, and re-layouts  0.72 us (1%)
    pallas_call x1, Pallas kernels, shards(): pl.pallas_call(kernel, out_shape=jax.ShapeDtypeStruct((1, 12, taus, width...  62.1 us

profile of v3, /device:TPU:16, one launch (start us, length us, event | category | flops | bytes accessed | tf_op | source)
XLA Modules:
  0.0 62.8 jit_solution(8779523326843396191)
XLA Ops:
  0.0 62.1 %shard_map.55 = f32[1,12,16,384]{3,2,1,0:T(8,128)S(1)} custom-call(s32[16,64]{1,0:T(8,128)} %bitcast.3, s32[2]{0:T(128)} %mom_hbm.1, f32[16,192]{1,0:T(8,128)} %energy_hbm.1, bf16[1,64,384]{2,1,0:T(8,128)(2,1)} %orb_ref.1, bf16[2,2,16,64,1024]{4,3,2,1,0:T(8,128)(2,1)} %w_hbm.1), custom_call_target="tpu_custom_call" | custom-call | tf_op jit(solution)/shard_map/pallas_call | solution.py:370
  62.1 0.7 %copy.7 = f32[1,16,12,384]{3,1,2,0:T(8,128)} copy(f32[1,16,12,384]{3,1,2,0:T(8,128)S(1)} %bitcast.2) | data formatting | bytes 589824

commit v4 on v3

--- a/solution.py
+++ b/solution.py
@@ -32,8 +32,8 @@
 
 
 def kernel(perm_hbm, mom_hbm, energy_hbm, orb_ref, w_hbm, out_ref,
-           perm_ref, mom_ref, energy_ref, own, xs, kg, wv, scr, lsc, hsend, hrecv, xkt, order, occ,
-           rsend, rrecv, fsend, frecv,
+           perm_ref, mom_ref, energy_ref, own, xs, kg, wv, scr, lsc, hsend, hrecv, xkt, order, unorder, occ,
+           rsend, rrecv, fsend, frecv, fwait,
            gsend, grecv, ksend, krecv, kcore, hss, hrs, rss, rrs, fss, frs, wsem, osem):
     g = lax.axis_index("kgrp")
     w = lax.axis_index("wrow")
@@ -145,14 +145,17 @@
     ktake(3, h)
     ktake(2, h)
     grelay(0, 0)
+    row = lax.broadcasted_iota(jnp.int32, (96, 96), 0)
+    col = lax.broadcasted_iota(jnp.int32, (96, 96), 1)
+    part, inner = lax.div(row, 24), lax.rem(row, 24)
+    split = lax.div(inner, 12) * 48 + part * 12 + lax.rem(inner, 12)
+    order[...] = jnp.where(col == split, 1.0, 0.0).astype(jnp.bfloat16)
     row = lax.broadcasted_iota(jnp.int32, (192, 192), 0)
     col = lax.broadcasted_iota(jnp.int32, (192, 192), 1)
-    part, inner = lax.div(row, 48), lax.rem(row, 48)
-    split = lax.div(inner, 12) * 48 + part * 12 + lax.rem(inner, 12)
     tau_row = lax.rem(row, 16)
-    merge = lax.rem(tau_row, 4) * 48 + lax.div(tau_row, 4) * 12 + lax.div(row, 16)
-    order[0] = jnp.where(col == split, 1.0, 0.0).astype(jnp.bfloat16)
-    order[1] = jnp.where(col == merge, 1.0, 0.0).astype(jnp.bfloat16)
+    late, odd = lax.div(tau_row, 8), lax.rem(lax.div(tau_row, 4), 2)
+    merge = late * 96 + lax.rem(tau_row, 4) * 24 + odd * 12 + lax.div(row, 16)
+    unorder[...] = jnp.where(col == merge, 1.0, 0.0).astype(jnp.bfloat16)
     for table in tables:
         table.wait()
     own_row = perm_ref[pl.ds(g, 1), :]
@@ -164,6 +167,9 @@
     kpass(mine)
     gforward(0, 1)
     gforward(0, 3)
+    ktake(1, 1 - h)
+    ktake(3, 1 - h)
+    ktake(2, 1 - h)
     gforward(0, 2)
     gfinish(0, 0)
     row = lax.broadcasted_iota(jnp.int32, (width, width), 0)
@@ -172,11 +178,7 @@
     pick = jnp.where(want == col, 1.0, 0.0).astype(jnp.bfloat16)
     strip = xs[0, pl.ds(z * 4, 4)].reshape(4 * rows, width)
     xkt[...] = lax.dot_general(pick, strip, NT, preferred_element_type=jnp.float32).astype(jnp.bfloat16)
-    ktake(1, 1 - h)
-    ktake(3, 1 - h)
-    ktake(2, 1 - h)
     grelay(0, 1)
-    grelay(0, 3)
     pltpu.make_async_remote_copy(
         src_ref=kg.at[pl.ds(0, 8)], dst_ref=kg.at[pl.ds(0, 8)], send_sem=ksend.at[0],
         recv_sem=kcore.at[0], device_id=(partner, w), device_id_type=MESH).wait_recv()
@@ -213,6 +215,7 @@
         return carry
 
     lax.fori_loop(0, 4, left_round, 0, unroll=True)
+    grelay(0, 3)
     grelay(0, 2)
 
     def screen(q, n, r):
@@ -256,21 +259,21 @@
     grelay(1, 3)
     gforward(2, 1)
     gforward(2, 3)
+    grelay(1, 2)
     gforward(2, 2)
-    grelay(1, 2)
-    gfinish(1, 1)
-    tile(0, 1)
-    gfinish(1, 3)
-    tile(0, 3)
-    grelay(2, 1)
-    grelay(2, 3)
-    gfinish(1, 2)
-    tile(0, 2)
-    grelay(2, 2)
     for i in range(2):
         pltpu.make_async_copy(w_hbm.at[1, i], wv.at[1, i], wsem.at[2 + i]).wait()
     gfinish(2, 0)
     tile(1, 0)
+    gfinish(1, 1)
+    grelay(2, 1)
+    tile(0, 1)
+    grelay(2, 3)
+    gfinish(1, 3)
+    tile(0, 3)
+    grelay(2, 2)
+    gfinish(1, 2)
+    tile(0, 2)
     gfinish(2, 1)
     tile(1, 1)
     gfinish(2, 3)
@@ -302,8 +305,8 @@
     def rcopy(r, d):
         other = wrap(z + d)
         return pltpu.make_async_remote_copy(
-            src_ref=rsend.at[r, other], dst_ref=rrecv.at[r, z], send_sem=rss.at[0],
-            recv_sem=rrs.at[0], device_id=(g, wdev(other, x)), device_id_type=MESH)
+            src_ref=rsend.at[r, other], dst_ref=rrecv.at[r, d - 1], send_sem=rss.at[0],
+            recv_sem=rrs.at[r // 2], device_id=(g, wdev(other, x)), device_id_type=MESH)
 
     def project(r):
         pltpu.make_async_remote_copy(
@@ -317,27 +320,30 @@
         for d in (2, 1, 3):
             rcopy(r, d).start()
 
-    for r in range(4):
-        project(r)
-
-    pltpu.make_async_remote_copy(
-        src_ref=rrecv.at[pl.ds(0, 3)], dst_ref=rrecv.at[pl.ds(0, 3)], send_sem=rss.at[0],
-        recv_sem=rrs.at[0], device_id=(g, right), device_id_type=MESH).wait_recv()
-    sums = []
-    for r in range(4):
-        total = rsend[r, z].astype(jnp.float32)
-        for d in range(1, 4):
-            total = total + rrecv[r, wrap(z + d)].astype(jnp.float32)
-        sums.append(total)
-    summed = jnp.concatenate(sums, axis=0).astype(jnp.bfloat16)
-    pieces = lax.dot_general(order[0], summed, NN, preferred_element_type=jnp.float32)
-    fsend[...] = pieces.astype(jnp.bfloat16).reshape(4, 48, width)
-    frecv[x] = fsend[x]
-    for e in (2, 1, 3):
-        other = wrap(x + e)
+    project(0)
+    project(1)
+    project(2)
+    project(3)
+
+    for part in range(2):
         pltpu.make_async_remote_copy(
-            src_ref=fsend.at[other], dst_ref=frecv.at[x], send_sem=fss.at[0],
-            recv_sem=frs.at[0], device_id=(g, wdev(z, other)), device_id_type=MESH).start()
+            src_ref=rrecv.at[pl.ds(2 * part, 2)], dst_ref=rrecv.at[pl.ds(2 * part, 2)], send_sem=rss.at[0],
+            recv_sem=rrs.at[part], device_id=(g, right), device_id_type=MESH).wait_recv()
+        sums = []
+        for r in (2 * part, 2 * part + 1):
+            total = rsend[r, z].astype(jnp.float32)
+            for i in range(3):
+                total = total + rrecv[r, i].astype(jnp.float32)
+            sums.append(total)
+        summed = jnp.concatenate(sums, axis=0).astype(jnp.bfloat16)
+        pieces = lax.dot_general(order[...], summed, NN, preferred_element_type=jnp.float32)
+        fsend[part] = pieces.reshape(4, 24, width).astype(jnp.bfloat16)
+        frecv[part, x] = fsend[part, x]
+        for e in (2, 1, 3):
+            other = wrap(x + e)
+            pltpu.make_async_remote_copy(
+                src_ref=fsend.at[part, other], dst_ref=frecv.at[part, x], send_sem=fss.at[0],
+                recv_sem=frs.at[0], device_id=(g, wdev(z, other)), device_id_type=MESH).start()
 
     for s in range(3):
         pltpu.make_async_remote_copy(
@@ -350,12 +356,13 @@
         src_ref=hsend.at[pl.ds(0, 3)], dst_ref=hrecv.at[pl.ds(0, 3)], send_sem=hss.at[0],
         recv_sem=hrs.at[0], device_id=(g, right), device_id_type=MESH).wait_send()
     pltpu.make_async_remote_copy(
-        src_ref=rsend.at[pl.ds(0, 3)], dst_ref=rrecv.at[pl.ds(0, 3)], send_sem=rss.at[0],
+        src_ref=rrecv, dst_ref=rrecv, send_sem=rss.at[0],
         recv_sem=rrs.at[0], device_id=(g, right), device_id_type=MESH).wait_send()
     pltpu.make_async_remote_copy(
-        src_ref=fsend.at[pl.ds(0, 3)], dst_ref=frecv.at[pl.ds(0, 3)], send_sem=fss.at[0],
+        src_ref=fwait, dst_ref=fwait, send_sem=fss.at[0],
         recv_sem=frs.at[0], device_id=(g, right), device_id_type=MESH).wait()
-    result = lax.dot_general(order[1], frecv[...].reshape(192, width), NN,
+    rows_in = frecv[...].astype(jnp.float32).reshape(192, width).astype(jnp.bfloat16)
+    result = lax.dot_general(unorder[...], rows_in, NN,
                              preferred_element_type=jnp.float32)
     out_ref[0] = unpack_columns(result).reshape(12, 16, width)
 
@@ -385,14 +392,16 @@
             pltpu.VMEM((4, 4, rows, width), bf16),
             pltpu.VMEM((4, 4, rows, width), bf16),
             pltpu.VMEM((width, 4 * rows), bf16),
-            pltpu.VMEM((2, 192, 192), bf16),
+            pltpu.VMEM((96, 96), bf16),
+            pltpu.VMEM((192, 192), bf16),
             pltpu.VMEM((2, taus, width), f32),
             pltpu.VMEM((4, 4, 48, width), bf16),
-            pltpu.VMEM((4, 4, 48, width), bf16),
-            pltpu.VMEM((4, 48, width), bf16),
-            pltpu.VMEM((4, 48, width), bf16),
+            pltpu.VMEM((4, 3, 48, width), bf16),
+            pltpu.VMEM((2, 4, 24, width), bf16),
+            pltpu.VMEM((2, 4, 24, width), bf16),
+            pltpu.VMEM((6, 24, width), bf16),
             dma((3,)), dma((3, 16)), dma((1,)), dma((16,)), dma((1,)),
-            dma((1,)), dma((4,)), dma((1,)), dma((1,)), dma((1,)), dma((1,)),
+            dma((1,)), dma((4,)), dma((1,)), dma((2,)), dma((1,)), dma((1,)),
             dma((4,)), dma((4,)),
         ],
         compiler_params=pltpu.CompilerParams(collective_id=0, has_side_effects=True, vmem_limit_bytes=40 * 2**20),

time: 63 us -> 61.9 us (0.983); the launches traced: 62.8 us -> 61 us
  Pallas kernels: 62.1 us -> 60.3 us
    pallas_call x1, Pallas kernels: 62.1 us -> 60.3 us  [shards(): pl.pallas_call(kernel, out_shape=jax.ShapeDtypeStruct((1, 12, taus, width...]
where the time goes in v4:
time: 61.9 us; the launch traced here: 61 us
  Pallas kernels  60.3 us (97%)
  local copies, waits for them, and re-layouts  0.72 us (1%)
    pallas_call x1, Pallas kernels, shards(): pl.pallas_call(kernel, out_shape=jax.ShapeDtypeStruct((1, 12, taus, width...  60.3 us

profile of v4, /device:TPU:16, one launch (start us, length us, event | category | flops | bytes accessed | tf_op | source)
XLA Modules:
  0.0 61.0 jit_solution(11908659569876605731)
XLA Ops:
  0.0 60.3 %shard_map.55 = f32[1,12,16,384]{3,2,1,0:T(8,128)S(1)} custom-call(s32[16,64]{1,0:T(8,128)} %bitcast.3, s32[2]{0:T(128)} %mom_hbm.1, f32[16,192]{1,0:T(8,128)} %energy_hbm.1, bf16[1,64,384]{2,1,0:T(8,128)(2,1)} %orb_ref.1, bf16[2,2,16,64,1024]{4,3,2,1,0:T(8,128)(2,1)} %w_hbm.1), custom_call_target="tpu_custom_call" | custom-call | tf_op jit(solution)/shard_map/pallas_call | solution.py:377
  60.3 0.7 %copy.7 = f32[1,16,12,384]{3,1,2,0:T(8,128)} copy(f32[1,16,12,384]{3,1,2,0:T(8,128)S(1)} %bitcast.2) | data formatting | bytes 589824
